TPU v7x, 256 devices: a whole 4x4x8 slice. The times are simulated.
256 devices in a mesh: dp: 16 (over z, y_hi), blk: 16 (over y_lo, x, core).
Axes of the slice: x: 4, y: 4 (y_hi: 2, y_lo: 2; y = y_hi * 2 + y_lo), z: 8, core: 2. Of those that a mesh axis runs over, the one named last changes fastest.
Arguments:
- q_raw: bfloat16 [16, 2048, 1536], P('dp', 'blk'), may hold values from -120 to 120
- q_tan: bfloat16 [16, 2048, 1536], P('dp', 'blk'), may hold values from -6 to 6
- k_raw: bfloat16 [16, 2048, 1536], P('dp', 'blk'), may hold values from -120 to 120
- k_tan: bfloat16 [16, 2048, 1536], P('dp', 'blk'), may hold values from -6 to 6
- values: bfloat16 [16, 2048, 1536], P('dp', 'blk'), may hold values from -6 to 6
- values_tan: bfloat16 [16, 2048, 1536], P('dp', 'blk'), may hold values from -6 to 6
- head_scale: float32 [12], replicated, may hold values from 1 to 3
- w_out: bfloat16 [1536, 1536], P('dp'), may hold values from -0.15625 to 0.15625
- gate: float32 [16, 1536], P('dp'), may hold values from 0.5 to 1.5
- gate_tan: float32 [16, 1536], P('dp'), may hold values from -4 to 4
Outputs:
- layer_out: bfloat16 [16, 2048, 1536], P('dp', 'blk')
- layer_tan: bfloat16 [16, 2048, 1536], P('dp', 'blk')
All inputs are finite; a program needn't handle non-finite values.
Results may differ from a plain program's by a relative error of at most 0.012.
Values may be sent and summed in bfloat16 or wider, within the bound.
A program may use at most 128 MiB of HBM per device.

v0:
```python
import math
import jax
import jax.numpy as jnp
from jax import lax
from jax.sharding import PartitionSpec as P

HEADS = 12
HEAD = 128
HD = 1536
epsilon = 1e-06


def normalize(raw_rows, tan_rows):
    shape = raw_rows.shape[:-1] + (HEADS, HEAD)
    direct = raw_rows.astype(jnp.float32).reshape(shape)
    moving = tan_rows.astype(jnp.float32).reshape(shape)
    recip = lax.rsqrt(jnp.mean(direct * direct, -1, keepdims=True) + epsilon)
    normed = direct * recip
    normed_tan = recip * (moving - normed * jnp.mean(normed * moving, -1, keepdims=True))
    return (normed.astype(jnp.bfloat16), normed_tan.astype(jnp.bfloat16))


def score_pair(q_norm, q_pair, key_flat, key_tan_flat, score_scale):
    count = key_flat.shape[0]
    key_norm = key_flat.reshape(count, HEADS, HEAD)
    key_pair = jnp.concatenate([key_norm, key_tan_flat.reshape(count, HEADS, HEAD)], -1)
    scores = (
        jnp.einsum("qhe,khe->qhk", q_norm, key_norm, preferred_element_type=jnp.float32)
        * score_scale
    )
    slopes = (
        jnp.einsum("qhe,khe->qhk", q_pair, key_pair, preferred_element_type=jnp.float32)
        * score_scale
    )
    return (scores, slopes)


def shards(q_raw, q_tan, k_raw, k_tan, values, values_tan, head_scale, w_out, gate, gate_tan):
    rows = q_raw.shape[1]
    q_norm, q_dir = normalize(q_raw[0], q_tan[0])
    k_norm, k_dir = normalize(k_raw[0], k_tan[0])
    key_flat = k_norm.reshape(rows, HD)
    key_tan_flat = k_dir.reshape(rows, HD)
    val_flat = values[0]
    val_tan_flat = values_tan[0]
    score_scale = (head_scale / math.sqrt(HEAD))[None, :, None]
    q_pair = jnp.concatenate([q_dir, q_norm], -1)
    all_keys, all_vals = (
        lax.all_gather(key_flat, "blk", axis=0, tiled=True),
        lax.all_gather(val_flat, "blk", axis=0, tiled=True),
    )
    whole_count = all_keys.shape[0]
    all_scores = (
        jnp.einsum(
            "qhe,khe->qhk",
            q_norm,
            all_keys.reshape(whole_count, HEADS, HEAD),
            preferred_element_type=jnp.float32,
        )
        * score_scale
    )
    all_probs = jnp.exp(all_scores)
    totals = jnp.sum(all_probs, -1)
    mixed = jnp.einsum(
        "qhk,khe->qhe",
        all_probs.astype(jnp.bfloat16),
        all_vals.reshape(whole_count, HEADS, HEAD),
        preferred_element_type=jnp.float32,
    )
    pieces = (
        lax.all_gather(key_tan_flat, "blk", axis=0, tiled=True),
        lax.all_gather(val_tan_flat, "blk", axis=0, tiled=True),
    )
    count = pieces[0].shape[0]
    val_part = all_vals.reshape(count, HEADS, HEAD)
    scores, slopes = score_pair(q_norm, q_pair, all_keys, pieces[0], score_scale)
    probs = jnp.exp(scores)
    prob_half = probs.astype(jnp.bfloat16)
    slope_half = (probs * slopes).astype(jnp.bfloat16)
    val_tan = pieces[1].reshape(count, HEADS, HEAD)
    more_tan = jnp.einsum("qhk,khe->qhe", slope_half, val_part, preferred_element_type=jnp.float32)
    more_tan = more_tan + jnp.einsum(
        "qhk,khe->qhe", prob_half, val_tan, preferred_element_type=jnp.float32
    )
    moments = jnp.sum(probs * slopes, -1)
    attended = (mixed / totals[..., None]).astype(jnp.bfloat16).reshape(rows, HD)
    attended_tan = (
        more_tan / totals[..., None] - mixed * moments[..., None] / (totals * totals)[..., None]
    )
    attended_tan = attended_tan.astype(jnp.bfloat16).reshape(rows, HD)
    stacked = jnp.concatenate([attended, attended_tan], 0)
    projected = jnp.dot(
        stacked, lax.all_gather(w_out, "dp", axis=0, tiled=True), preferred_element_type=jnp.float32
    )
    gate_row = gate[0][None, :]
    gate_tan_row = gate_tan[0][None, :]
    layer_out = (gate_row * projected[:rows]).astype(jnp.bfloat16)
    layer_tan = (gate_tan_row * projected[:rows] + gate_row * projected[rows:]).astype(jnp.bfloat16)
    return (layer_out[None], layer_tan[None])


def solution(mesh):
    return jax.shard_map(
        shards,
        mesh=mesh,
        in_specs=(
            P("dp", "blk", None),
            P("dp", "blk", None),
            P("dp", "blk", None),
            P("dp", "blk", None),
            P("dp", "blk", None),
            P("dp", "blk", None),
            P(),
            P("dp", None),
            P("dp", None),
            P("dp", None),
        ),
        out_specs=(P("dp", "blk", None), P("dp", "blk", None)),
        check_vma=False,
    )
```

profile of v0, /device:TPU:2, one launch (start us, length us, event | category | flops | bytes accessed | tf_op | source)
XLA Modules:
  0.0 339.6 jit_solution(3919737039438799846)
XLA Ops:
  7.3 1.3 copy.19
  8.5 0.1 multiply_reduce_fusion.3
  8.7 1.2 copy.25
  9.9 0.1 multiply_reduce_fusion.1
  10.0 1.1 fusion.23
  11.2 0.7 all-gather.10.cloned.1.call-update
  11.9 0.7 all-gather.14.cloned.1.call-update
  12.7 0.5 all-gather.16.cloned.1.call-update
  13.2 0.5 all-gather.12.cloned.1.call-update
  13.8 0.2 copy.20
  14.0 0.2 copy.21
  14.2 0.2 copy.28
  14.4 0.2 copy.30
  14.7 0.1 multiply_reduce_fusion.2
  14.8 0.5 multiply_reduce_fusion
  15.4 0.5 multiply_convert_fusion.1
  15.9 55.1 %all-gather.8.cloned.1.call-done = bf16[2048,1536]{0,1:T(8,128)(2,1)} async-done(((bf16[128,1536]{0,1:T(8,128)(2,1)}), bf16[2048,1536]{0,1:T(8,128)(2,1)}) %all-gather.8.cloned.1.call-update) | async-done | bytes 6291472 | tf_op jit(solution)/shard_map/all_gather | solution.py:49
  70.9 8.7 %copy.26 = bf16[2048,12,128]{2,0,1:T(8,128)(2,1)} copy(bf16[2048,12,128]{0,2,1:T(8,128)(2,1)} %bitcast.68) | data formatting | bytes 12582912 | tf_op jit(solution)/shard_map/reshape | solution.py:57
  79.6 48.6 %all-gather.10.cloned.1.call-done = bf16[2048,1536]{0,1:T(8,128)(2,1)} async-done(((bf16[128,1536]{0,1:T(8,128)(2,1)}), bf16[2048,1536]{0,1:T(8,128)(2,1)}) %all-gather.10.cloned.1.call-update) | async-done | bytes 6291472 | tf_op jit(solution)/shard_map/all_gather | solution.py:71
  128.2 8.6 %copy.27 = bf16[2048,12,128]{2,0,1:T(8,128)(2,1)} copy(bf16[2048,12,128]{0,2,1:T(8,128)(2,1)} %bitcast.75) | data formatting | bytes 12582912 | tf_op jit(solution)/shard_map/reshape | solution.py:26
  136.8 10.8 %bitcast_reduce_fusion = (f32[128,12]{0,1:T(8,128)S(1)}, f32[12,2048,128]{2,1,0:T(8,128)}) fusion(f32[12]{0:T(128)S(1)} %broadcast_multiply_fusion.2, bf16[2048,12,128]{0,2,1:T(8,128)(2,1)} %bitcast.69, bf16[128,12,128]{2,0,1:T(8,128)(2,1)S(1)} %get-tuple-element.7), kind=kOutput, calls=%fused_computation.5 | convolution fusion | flops 811596288 | bytes 19273776 | tf_op jit(solution)/shard_map/qhe,khe->qhk/dot_general | solution.py:54
  147.6 25.5 %all-gather.14.cloned.1.call-done = bf16[1,2048,1536]{2,1,0:T(8,128)(2,1)} async-done(((bf16[1,128,1536]{2,1,0:T(8,128)(2,1)}), bf16[1,2048,1536]{2,1,0:T(8,128)(2,1)}) %all-gather.14.cloned.1.call-update) | async-done | bytes 6291472 | tf_op jit(solution)/shard_map/all_gather | solution.py:50
  173.1 8.6 %copy.23 = bf16[1,2048,1536]{1,2,0:T(8,128)(2,1)} copy(bf16[1,2048,1536]{2,1,0:T(8,128)(2,1)} %all-gather.14.cloned.1.call-done) | data formatting | bytes 12582912 | tf_op jit(solution)/shard_map/all_gather | solution.py:50
  181.7 38.8 %all-gather.16.cloned.1.call-done = bf16[1,2048,1536]{2,1,0:T(8,128)(2,1)} async-done(((bf16[1,128,1536]{2,1,0:T(8,128)(2,1)}), bf16[1,2048,1536]{2,1,0:T(8,128)(2,1)}) %all-gather.16.cloned.1.call-update) | async-done | bytes 6291472 | tf_op jit(solution)/shard_map/all_gather | solution.py:72
  220.5 8.9 %copy.32 = bf16[1,2048,1536]{1,2,0:T(8,128)(2,1)} copy(bf16[1,2048,1536]{2,1,0:T(8,128)(2,1)} %all-gather.16.cloned.1.call-done) | data formatting | bytes 12582912 | tf_op jit(solution)/shard_map/all_gather | solution.py:72
  229.4 9.1 %fusion.39 = f32[12,128,128]{1,2,0:T(8,128)S(1)} fusion(bf16[2048,12,128]{0,2,1:T(8,128)(2,1)} %bitcast.74, f32[12,2048,128]{2,1,0:T(8,128)} %get-tuple-element.11, f32[12]{0:T(128)S(1)} %broadcast_multiply_fusion.2), kind=kOutput, calls=%fused_computation.49 | convolution fusion | flops 811597824 | bytes 19660848 | tf_op jit(solution)/shard_map/qhk,khe->qhe/dot_general | solution.py:82
  238.6 7.3 %divide_convert_fusion = (bf16[128,12,128]{0,2,1:T(8,128)(2,1)S(1)}, f32[128,12,128]{0,2,1:T(8,128)S(1)}) fusion(f32[128,12]{0,1:T(8,128)S(1)} %get-tuple-element.10, bf16[2048,12,128]{0,2,1:T(8,128)(2,1)S(1)} %bitcast.72, f32[12,2048,128]{2,1,0:T(8,128)} %get-tuple-element.11, f32[12]{0:T(128)S(1)} %broadcast_multiply_fusion.2), kind=kOutput, calls=%fused_computation.35 | convolution fusion | flops 811991040 | bytes 20060208 | tf_op jit(solution)/shard_map/qhk,khe->qhe/dot_general | solution.py:64
  245.9 13.0 %fusion.40 = (f32[128,12]{0,1:T(8,128)S(1)}, bf16[128,12,2048]{0,2,1:T(8,128)(2,1)}) fusion(bf16[128,12,128]{2,0,1:T(8,128)(2,1)S(1)} %get-tuple-element.7, bf16[128,12,128]{2,0,1:T(8,128)(2,1)S(1)} %get-tuple-element.6, bf16[2048,12,128]{2,0,1:T(8,128)(2,1)} %copy.27, bf16[2048,12,128]{2,0,1:T(8,128)(2,1)} %copy.26, ...), kind=kOutput, calls=%fused_computation.50 | convolution fusion | flops 1653078528 | bytes 32249904 | tf_op jit(solution)/shard_map/qhe,khe->qhk/dot_general | solution.py:32
  258.9 4.6 %fusion.20 = bf16[128,12,128]{0,2,1:T(8,128)(2,1)S(1)} fusion(f32[12,128,128]{1,2,0:T(8,128)S(1)} %fusion.39, bf16[2048,12,128]{0,2,1:T(8,128)(2,1)S(1)} %bitcast.73, bf16[128,12,2048]{0,2,1:T(8,128)(2,1)} %get-tuple-element.13, f32[128,12,128]{0,2,1:T(8,128)S(1)} %get-tuple-element.15, f32[128,12]{0,1:T(8,128)S(1)} %mul.183, ...), kind=kOutput, calls=%fused_computation.17 | convolution fusion | flops 806486016 | bytes 14567424 | tf_op jit(solution)/shard_map/qhk,khe->qhe/dot_general | solution.py:81
  263.5 64.7 %all-gather.12.cloned.1.call-done = bf16[1536,1536]{1,0:T(8,128)(2,1)} async-done(((bf16[96,1536]{1,0:T(8,128)(2,1)}), bf16[1536,1536]{1,0:T(8,128)(2,1)}) %all-gather.12.cloned.1.call-update) | async-done | bytes 4718608 | tf_op jit(solution)/shard_map/all_gather | solution.py:93
  328.3 3.7 %fusion.29 = f32[256,1536]{1,0:T(8,128)S(1)} fusion(bf16[1536,1536]{1,0:T(8,128)(2,1)} %all-gather.12.cloned.1.call-done, bf16[128,1536]{0,1:T(8,128)(2,1)S(1)} %bitcast.82, bf16[128,1536]{0,1:T(8,128)(2,1)S(1)} %bitcast.81), kind=kOutput, calls=%fused_computation.25 | convolution fusion | flops 1209532416 | bytes 7077888 | tf_op jit(solution)/shard_map/dot_general | solution.py:92
  332.0 1.0 fusion.36
  (29 shorter events, 0.3 us)
Async XLA Ops:
  7.2 6.6 %copy-start = (bf16[1,128,1536]{2,1,0:T(8,128)(2,1)S(1)}, bf16[1,128,1536]{2,1,0:T(8,128)(2,1)}, u32[]{:S(2)}) copy-start(bf16[1,128,1536]{2,1,0:T(8,128)(2,1)} %param.10) | copy-start | bytes 1179652
  7.2 7.0 %copy-start.1 = (bf16[1,128,1536]{2,1,0:T(8,128)(2,1)S(1)}, bf16[1,128,1536]{2,1,0:T(8,128)(2,1)}, u32[]{:S(2)}) copy-start(bf16[1,128,1536]{2,1,0:T(8,128)(2,1)} %param.11) | copy-start | bytes 1179652
  7.2 7.5 %copy-start.2 = (f32[1,1536]{1,0:T(1,128)S(1)}, f32[1,1536]{1,0:T(1,128)}, u32[]{:S(2)}) copy-start(f32[1,1536]{1,0:T(1,128)} %param.18) | copy-start | bytes 18436
  7.2 7.5 %copy-start.3 = (f32[1,1536]{1,0:T(1,128)S(1)}, f32[1,1536]{1,0:T(1,128)}, u32[]{:S(2)}) copy-start(f32[1,1536]{1,0:T(1,128)} %param.19) | copy-start | bytes 18436
  7.2 63.7 %all-gather.8.cloned.1.call-start = ((), (), s32[]{:S(2)}) async-start(), calls=%async_computation | async-start | bytes 6684672 | tf_op jit(solution)/shard_map/all_gather | solution.py:49
  8.5 6.8 %copy-start.4 = (f32[12]{0:T(128)S(1)}, f32[12]{0:T(128)}, u32[]{:S(2)}) copy-start(f32[12]{0:T(128)} %param.16) | copy-start | bytes 148
  11.1 117.1 %all-gather.10.cloned.1.call-start = ((), (), s32[]{:S(2)}) async-start(), calls=%async_computation.1 | async-start | bytes 6684672 | tf_op jit(solution)/shard_map/all_gather | solution.py:71
  11.9 161.2 %all-gather.14.cloned.1.call-start = ((), (), s32[]{:S(2)}) async-start(), calls=%async_computation.3 | async-start | bytes 6684672 | tf_op jit(solution)/shard_map/all_gather | solution.py:50
  12.6 207.9 %all-gather.16.cloned.1.call-start = ((), (), s32[]{:S(2)}) async-start(), calls=%async_computation.4 | async-start | bytes 6684672 | tf_op jit(solution)/shard_map/all_gather | solution.py:72
  13.2 315.1 %all-gather.12.cloned.1.call-start = ((), (), s32[]{:S(2)}) async-start(), calls=%async_computation.2 | async-start | bytes 5013504 | tf_op jit(solution)/shard_map/all_gather | solution.py:93
  220.5 18.1 %slice-start = ((s8[6291456]{0:T(1024)(128)(4,1)}), s8[2097152]{0:T(1024)(128)(4,1)S(1)}, s32[]{:S(2)}) async-start(s8[6291456]{0:T(1024)(128)(4,1)} %bitcast.70), calls=%async_computation.5 | async-start | bytes 4194304
  229.4 9.2 %slice-start.1 = ((s8[6291456]{0:T(1024)(128)(4,1)}), s8[4194304]{0:T(1024)(128)(4,1)S(1)}, s32[]{:S(2)}) async-start(s8[6291456]{0:T(1024)(128)(4,1)} %bitcast.70), calls=%async_computation.6 | async-start | bytes 8388608
Sparse Core Ops, SparseCore 0:
  11.3 59.6 all-gather.7
  73.3 54.9 all-gather.9
  130.1 42.9 all-gather.13
  174.8 45.6 all-gather.15
  223.0 105.2 all-gather.11
where the time goes:
time: 341 us; the launch traced here: 340 us
  waiting for transfers between devices  235 us (69%)
  matrix products  48.5 us (14%)
  local copies, waits for them, and re-layouts  38.1 us (11%)
  between operations  14 us (4%)
  other arithmetic  3.49 us (1%)
    all_gather x1, waiting for transfers between devices, shards(): lax.all_gather(w_out, 'dp', axis=0, tiled=True)  64.7 us
    all_gather x1, waiting for transfers between devices, shards(): lax.all_gather(key_flat, 'blk', axis=0, tiled=True)  55.1 us
    all_gather x1, waiting for transfers between devices, shards(): lax.all_gather(key_tan_flat, 'blk', axis=0, tiled=True)  48.6 us
    all_gather x1, waiting for transfers between devices, shards(): lax.all_gather(val_tan_flat, 'blk', axis=0, tiled=True)  38.8 us
    all_gather x1, waiting for transfers between devices, shards(): lax.all_gather(val_flat, 'blk', axis=0, tiled=True)  25.5 us
    dot_general x1, matrix products, score_pair(): jnp.einsum('qhe,khe->qhk', q_pair, key_pair, preferred_element_type=jnp.f...  13 us
    dot_general x1, matrix products, shards(): jnp.einsum('qhe,khe->qhk', q_norm, all_keys.reshape(whole_count, HEADS, H...  10.8 us
    dot_general x1, matrix products, shards(): jnp.einsum('qhk,khe->qhe', prob_half, val_tan, preferred_element_type=jnp...  9.15 us
  transfers between devices with their start and end apart: 5, of which 5 were waited for; matrix products, arithmetic and copies ran while one was open for 24% of the time, Pallas kernels for 0%

commit v1 on v0

--- a/solution.py
+++ b/solution.py
@@ -90,7 +90,11 @@
     attended_tan = attended_tan.astype(jnp.bfloat16).reshape(rows, HD)
     stacked = jnp.concatenate([attended, attended_tan], 0)
     projected = jnp.dot(
-        stacked, lax.all_gather(w_out, "dp", axis=0, tiled=True), preferred_element_type=jnp.float32
+        stacked,
+        jnp.concatenate(
+            lax.all_to_all(jnp.stack([w_out] * lax.axis_size("dp")), "dp", 0, 0), axis=0
+        ),
+        preferred_element_type=jnp.float32,
     )
     gate_row = gate[0][None, :]
     gate_tan_row = gate_tan[0][None, :]

time: 341 us -> 314 us (0.921)
  waiting for transfers between devices: 235 us -> 193 us
  starting transfers between devices: 0.19 us -> 11.5 us
    all_gather x1 -> x0, waiting for transfers between devices: 64.7 us -> none  [shards(): lax.all_gather(w_out, 'dp', axis=0, tiled=True)]
    all_gather x1, waiting for transfers between devices: 48.6 us -> 79.5 us  [shards(): lax.all_gather(key_tan_flat, 'blk', axis=0, tiled=True)]
    all_gather x1, waiting for transfers between devices: 55.1 us -> 43.1 us  [shards(): lax.all_gather(key_flat, 'blk', axis=0, tiled=True)]
    all_to_all x0 -> x1, starting transfers between devices: none -> 11.4 us  [shards(): lax.all_to_all(jnp.stack([w_out] * lax.axis_size('dp')), 'dp', 0, 0)]
    all_gather x1, waiting for transfers between devices: 25.5 us -> 29.6 us  [shards(): lax.all_gather(val_flat, 'blk', axis=0, tiled=True)]
  transfers between devices with their start and end apart: 5 -> 5, of which waited for: 5 -> 4; matrix products, arithmetic and copies ran while one was open for 24% -> 27% of each run, Pallas kernels for 0% -> 0%
where the time goes in v1:
time: 314 us; the launch traced here: 311 us
  waiting for transfers between devices  193 us (61%)
  matrix products  48.6 us (15%)
  local copies, waits for them, and re-layouts  40.7 us (13%)
  between operations  14 us (4%)
  starting transfers between devices  11.5 us (4%)
  other arithmetic  3.49 us (1%)
    all_gather x1, waiting for transfers between devices, shards(): lax.all_gather(key_tan_flat, 'blk', axis=0, tiled=True)  79.5 us
    all_gather x1, waiting for transfers between devices, shards(): lax.all_gather(key_flat, 'blk', axis=0, tiled=True)  43.1 us
    all_gather x1, waiting for transfers between devices, shards(): lax.all_gather(val_tan_flat, 'blk', axis=0, tiled=True)  38.8 us
    all_gather x1, waiting for transfers between devices, shards(): lax.all_gather(val_flat, 'blk', axis=0, tiled=True)  29.6 us
    dot_general x1, matrix products, score_pair(): jnp.einsum('qhe,khe->qhk', q_pair, key_pair, preferred_element_type=jnp.f...  13.1 us
    all_to_all x1, starting transfers between devices, shards(): lax.all_to_all(jnp.stack([w_out] * lax.axis_size('dp')), 'dp', 0, 0)  11.4 us
    dot_general x1, matrix products, shards(): jnp.einsum('qhe,khe->qhk', q_norm, all_keys.reshape(whole_count, HEADS, H...  10.8 us
    dot_general x1, matrix products, shards(): jnp.einsum('qhk,khe->qhe', prob_half, val_tan, preferred_element_type=jnp...  9.13 us
  transfers between devices with their start and end apart: 5, of which 4 were waited for; matrix products, arithmetic and copies ran while one was open for 27% of the time, Pallas kernels for 0%

profile of v1, /device:TPU:2, one launch (start us, length us, event | category | flops | bytes accessed | tf_op | source)
XLA Modules:
  0.0 311.3 jit_solution(12842472336223844522)
XLA Ops:
  7.2 1.2 copy.19
  8.5 0.1 multiply_reduce_fusion.3
  8.6 1.2 copy.25
  9.8 0.1 multiply_reduce_fusion.1
  10.0 1.1 fusion.23
  11.1 0.7 all-gather.9.cloned.1.call-update
  11.9 0.7 all-gather.11.cloned.1.call-update
  12.6 0.5 all-gather.13.cloned.1.call-update
  13.2 2.6 stack.2
  15.7 11.4 %all-to-all-start = ((bf16[16,96,1536]{2,1,0:T(8,128)(2,1)}), bf16[16,96,1536]{2,1,0:T(8,128)(2,1)}, u32[]{:S(2)}, u32[]{:S(2)}) async-start(bf16[16,96,1536]{2,1,0:T(8,128)(2,1)} %stack.2), calls=%async_computation | async-start | bytes 9437184 | tf_op jit(solution)/shard_map/all_to_all | solution.py:95
  27.1 0.2 copy.20
  27.4 0.2 copy.21
  27.6 0.2 copy.28
  27.8 0.2 copy.30
  28.1 0.1 multiply_reduce_fusion.2
  28.2 0.5 multiply_reduce_fusion
  28.7 0.5 multiply_convert_fusion.1
  29.2 43.1 %all-gather.7.cloned.1.call-done = bf16[2048,1536]{0,1:T(8,128)(2,1)} async-done(((bf16[128,1536]{0,1:T(8,128)(2,1)}), bf16[2048,1536]{0,1:T(8,128)(2,1)}) %all-gather.7.cloned.1.call-update) | async-done | bytes 6291472 | tf_op jit(solution)/shard_map/all_gather | solution.py:49
  72.3 8.7 %copy.26 = bf16[2048,12,128]{2,0,1:T(8,128)(2,1)} copy(bf16[2048,12,128]{0,2,1:T(8,128)(2,1)} %bitcast.69) | data formatting | bytes 12582912 | tf_op jit(solution)/shard_map/reshape | solution.py:57
  81.0 79.5 %all-gather.9.cloned.1.call-done = bf16[2048,1536]{0,1:T(8,128)(2,1)} async-done(((bf16[128,1536]{0,1:T(8,128)(2,1)}), bf16[2048,1536]{0,1:T(8,128)(2,1)}) %all-gather.9.cloned.1.call-update) | async-done | bytes 6291472 | tf_op jit(solution)/shard_map/all_gather | solution.py:71
  160.5 8.6 %copy.27 = bf16[2048,12,128]{2,0,1:T(8,128)(2,1)} copy(bf16[2048,12,128]{0,2,1:T(8,128)(2,1)} %bitcast.76) | data formatting | bytes 12582912 | tf_op jit(solution)/shard_map/reshape | solution.py:26
  169.2 10.8 %bitcast_reduce_fusion = (f32[128,12]{0,1:T(8,128)S(1)}, f32[12,2048,128]{2,1,0:T(8,128)}) fusion(f32[12]{0:T(128)S(1)} %broadcast_multiply_fusion.2, bf16[2048,12,128]{0,2,1:T(8,128)(2,1)} %bitcast.70, bf16[128,12,128]{2,0,1:T(8,128)(2,1)S(1)} %get-tuple-element.7), kind=kOutput, calls=%fused_computation.5 | convolution fusion | flops 811596288 | bytes 19273776 | tf_op jit(solution)/shard_map/qhe,khe->qhk/dot_general | solution.py:54
  179.9 29.6 %all-gather.11.cloned.1.call-done = bf16[1,2048,1536]{2,1,0:T(8,128)(2,1)} async-done(((bf16[1,128,1536]{2,1,0:T(8,128)(2,1)}), bf16[1,2048,1536]{2,1,0:T(8,128)(2,1)}) %all-gather.11.cloned.1.call-update) | async-done | bytes 6291472 | tf_op jit(solution)/shard_map/all_gather | solution.py:50
  209.5 8.6 %copy.23 = bf16[1,2048,1536]{1,2,0:T(8,128)(2,1)} copy(bf16[1,2048,1536]{2,1,0:T(8,128)(2,1)} %all-gather.11.cloned.1.call-done) | data formatting | bytes 12582912 | tf_op jit(solution)/shard_map/all_gather | solution.py:50
  218.1 38.8 %all-gather.13.cloned.1.call-done = bf16[1,2048,1536]{2,1,0:T(8,128)(2,1)} async-done(((bf16[1,128,1536]{2,1,0:T(8,128)(2,1)}), bf16[1,2048,1536]{2,1,0:T(8,128)(2,1)}) %all-gather.13.cloned.1.call-update) | async-done | bytes 6291472 | tf_op jit(solution)/shard_map/all_gather | solution.py:72
  256.9 8.9 %copy.32 = bf16[1,2048,1536]{1,2,0:T(8,128)(2,1)} copy(bf16[1,2048,1536]{2,1,0:T(8,128)(2,1)} %all-gather.13.cloned.1.call-done) | data formatting | bytes 12582912 | tf_op jit(solution)/shard_map/all_gather | solution.py:72
  265.9 9.1 %fusion.39 = f32[12,128,128]{1,2,0:T(8,128)S(1)} fusion(bf16[2048,12,128]{0,2,1:T(8,128)(2,1)} %bitcast.75, f32[12,2048,128]{2,1,0:T(8,128)} %get-tuple-element.11, f32[12]{0:T(128)S(1)} %broadcast_multiply_fusion.2), kind=kOutput, calls=%fused_computation.49 | convolution fusion | flops 811597824 | bytes 19660848 | tf_op jit(solution)/shard_map/qhk,khe->qhe/dot_general | solution.py:82
  275.0 7.3 %divide_convert_fusion = (bf16[128,12,128]{0,2,1:T(8,128)(2,1)S(1)}, f32[128,12,128]{0,2,1:T(8,128)S(1)}) fusion(f32[128,12]{0,1:T(8,128)S(1)} %get-tuple-element.10, bf16[2048,12,128]{0,2,1:T(8,128)(2,1)S(1)} %bitcast.73, f32[12,2048,128]{2,1,0:T(8,128)} %get-tuple-element.11, f32[12]{0:T(128)S(1)} %broadcast_multiply_fusion.2), kind=kOutput, calls=%fused_computation.35 | convolution fusion | flops 811991040 | bytes 20060208 | tf_op jit(solution)/shard_map/qhk,khe->qhe/dot_general | solution.py:64
  282.3 13.1 %fusion.40 = (f32[128,12]{0,1:T(8,128)S(1)}, bf16[128,12,2048]{0,2,1:T(8,128)(2,1)}) fusion(bf16[128,12,128]{2,0,1:T(8,128)(2,1)S(1)} %get-tuple-element.7, bf16[128,12,128]{2,0,1:T(8,128)(2,1)S(1)} %get-tuple-element.6, bf16[2048,12,128]{2,0,1:T(8,128)(2,1)} %copy.27, bf16[2048,12,128]{2,0,1:T(8,128)(2,1)} %copy.26, ...), kind=kOutput, calls=%fused_computation.50 | convolution fusion | flops 1653078528 | bytes 32249904 | tf_op jit(solution)/shard_map/qhe,khe->qhk/dot_general | solution.py:32
  295.4 4.6 %fusion.20 = bf16[128,12,128]{0,2,1:T(8,128)(2,1)S(1)} fusion(f32[12,128,128]{1,2,0:T(8,128)S(1)} %fusion.39, bf16[2048,12,128]{0,2,1:T(8,128)(2,1)S(1)} %bitcast.74, bf16[128,12,2048]{0,2,1:T(8,128)(2,1)} %get-tuple-element.13, f32[128,12,128]{0,2,1:T(8,128)S(1)} %get-tuple-element.15, f32[128,12]{0,1:T(8,128)S(1)} %mul.183, ...), kind=kOutput, calls=%fused_computation.17 | convolution fusion | flops 806486016 | bytes 14567424 | tf_op jit(solution)/shard_map/qhk,khe->qhe/dot_general | solution.py:81
  300.0 3.7 %fusion.29 = f32[256,1536]{1,0:T(8,128)S(1)} fusion(bf16[1536,1536]{1,0:T(8,128)(2,1)} %bitcast.20, bf16[128,1536]{0,1:T(8,128)(2,1)S(1)} %bitcast.83, bf16[128,1536]{0,1:T(8,128)(2,1)S(1)} %bitcast.82), kind=kOutput, calls=%fused_computation.25 | convolution fusion | flops 1209532416 | bytes 7077888 | tf_op jit(solution)/shard_map/dot_general | solution.py:92
  303.7 1.0 fusion.36
  (31 shorter events, 0.3 us)
Async XLA Ops:
  7.2 6.0 %copy-start.2 = (bf16[96,1536]{1,0:T(8,128)(2,1)S(1)}, bf16[96,1536]{1,0:T(8,128)(2,1)}, u32[]{:S(2)}) copy-start(bf16[96,1536]{1,0:T(8,128)(2,1)} %param.17) | copy-start | bytes 884740
  7.2 65.1 %all-gather.7.cloned.1.call-start = ((), (), s32[]{:S(2)}) async-start(), calls=%async_computation.1 | async-start | bytes 6684672 | tf_op jit(solution)/shard_map/all_gather | solution.py:49
  11.1 149.5 %all-gather.9.cloned.1.call-start = ((), (), s32[]{:S(2)}) async-start(), calls=%async_computation.2 | async-start | bytes 6684672 | tf_op jit(solution)/shard_map/all_gather | solution.py:71
  11.8 197.7 %all-gather.11.cloned.1.call-start = ((), (), s32[]{:S(2)}) async-start(), calls=%async_computation.3 | async-start | bytes 6684672 | tf_op jit(solution)/shard_map/all_gather | solution.py:50
  12.6 244.4 %all-gather.13.cloned.1.call-start = ((), (), s32[]{:S(2)}) async-start(), calls=%async_computation.4 | async-start | bytes 6684672 | tf_op jit(solution)/shard_map/all_gather | solution.py:72
  13.1 14.0 %copy-start = (bf16[1,128,1536]{2,1,0:T(8,128)(2,1)S(1)}, bf16[1,128,1536]{2,1,0:T(8,128)(2,1)}, u32[]{:S(2)}) copy-start(bf16[1,128,1536]{2,1,0:T(8,128)(2,1)} %param.10) | copy-start | bytes 1179652
  15.7 11.8 %copy-start.1 = (bf16[1,128,1536]{2,1,0:T(8,128)(2,1)S(1)}, bf16[1,128,1536]{2,1,0:T(8,128)(2,1)}, u32[]{:S(2)}) copy-start(bf16[1,128,1536]{2,1,0:T(8,128)(2,1)} %param.11) | copy-start | bytes 1179652
  15.7 12.3 %copy-start.3 = (f32[1,1536]{1,0:T(1,128)S(1)}, f32[1,1536]{1,0:T(1,128)}, u32[]{:S(2)}) copy-start(f32[1,1536]{1,0:T(1,128)} %param.18) | copy-start | bytes 18436
  15.7 12.3 %copy-start.4 = (f32[1,1536]{1,0:T(1,128)S(1)}, f32[1,1536]{1,0:T(1,128)}, u32[]{:S(2)}) copy-start(f32[1,1536]{1,0:T(1,128)} %param.19) | copy-start | bytes 18436
  15.7 13.0 %copy-start.5 = (f32[12]{0:T(128)S(1)}, f32[12]{0:T(128)}, u32[]{:S(2)}) copy-start(f32[12]{0:T(128)} %param.16) | copy-start | bytes 148
  15.7 284.3 %all-to-all-start = ((bf16[16,96,1536]{2,1,0:T(8,128)(2,1)}), bf16[16,96,1536]{2,1,0:T(8,128)(2,1)}, u32[]{:S(2)}, u32[]{:S(2)}) async-start(bf16[16,96,1536]{2,1,0:T(8,128)(2,1)} %stack.2), calls=%async_computation | async-start | bytes 9437184 | tf_op jit(solution)/shard_map/all_to_all | solution.py:95
  256.9 18.1 %slice-start = ((s8[6291456]{0:T(1024)(128)(4,1)}), s8[2097152]{0:T(1024)(128)(4,1)S(1)}, s32[]{:S(2)}) async-start(s8[6291456]{0:T(1024)(128)(4,1)} %bitcast.71), calls=%async_computation.5 | async-start | bytes 4194304
  265.8 9.1 %slice-start.1 = ((s8[6291456]{0:T(1024)(128)(4,1)}), s8[4194304]{0:T(1024)(128)(4,1)S(1)}, s32[]{:S(2)}) async-start(s8[6291456]{0:T(1024)(128)(4,1)} %bitcast.71), calls=%async_computation.6 | async-start | bytes 8388608
Sparse Core Ops, SparseCore 0:
  11.2 61.0 all-gather.6
  74.7 85.8 all-gather.8
  162.4 47.0 all-gather.10
  211.2 45.6 all-gather.12
